TPU v7x, 512 devices: a whole 4x4x16 slice. The times are simulated.
512 devices in a mesh: mp: 64 (over x, z), replica: 8 (over y, core).
Axes of the slice: x: 4, y: 4, z: 16, core: 2. Of those that a mesh axis runs over, the one named last changes fastest.
Arguments:
- pooled_grads: bfloat16 [64, 8, 128, 64, 128], P('mp', 'replica'), may hold values from -0.119628906 to 0.119628906
- table: float32 [64, 512, 128], P('mp'), may hold values from -3 to 3
- state: float32 [64, 512], P('mp'), may hold values from 0.2 to 5
- tile_mult: bfloat16 [64, 8, 64, 128, 128], P('mp', 'replica'), may hold values from 0 to 3, as said below
- tile_rows: int32 [64, 8, 64], P('mp', 'replica'), may hold values from 0 to 3
Outputs:
- new_table: float32 [64, 512, 128], P('mp')
- new_state: float32 [64, 512], P('mp')
Inputs may be any that keep to these rules, and one draw needn't show every extreme that they name: tile_mult holds whole numbers.
All inputs are finite; a program needn't handle non-finite values.
Results may differ from a plain program's by a relative error of at most 0.0003.
Values may be sent and summed in bfloat16 or wider, within the bound.
No kernel may reach another device: no remote copies, remote signals or barrier semaphores. Data moves between devices by JAX's collectives and lax.ppermute only.
A program may use at most 64 MiB of HBM per device.

v0:
```python
import jax
import jax.numpy as jnp
from jax import lax
from jax.sharding import PartitionSpec as P

LEARN_RATE = 0.5
EPSILON = 1e-06


def adagrad(weights_in, accum_in, gradient):
    accum_out = accum_in + jnp.mean(gradient * gradient, axis=-1)
    weights_out = weights_in - LEARN_RATE * gradient / (jnp.sqrt(accum_out)[..., None] + EPSILON)
    return (weights_out, accum_out)


def on_device(pooled_grads, table, state, tile_mult, tile_rows):
    local_grads = pooled_grads[0, 0]
    width = local_grads.shape[-1]
    received = lax.all_to_all(local_grads, "mp", split_axis=1, concat_axis=0, tiled=True)
    counts_bf = tile_mult[0, 0]
    block_size = counts_bf.shape[-1]
    sample_blocks = received.reshape(-1, block_size, width)
    row_ids = tile_rows[0, 0]
    contrib = jnp.einsum(
        "tsr,tse->tre", counts_bf, sample_blocks, preferred_element_type=jnp.float32
    )
    weights_in = table[0]
    accum_in = state[0]
    row_count = weights_in.shape[0]
    row_blocks = row_count // block_size
    onehot = (row_ids[:, None] == jnp.arange(row_blocks, dtype=jnp.int32)[None, :]).astype(
        jnp.float32
    )
    partial_grad = jnp.einsum(
        "tb,tre->bre", onehot, contrib, precision=lax.Precision.HIGHEST
    ).reshape(row_count, width)
    total_grad = lax.psum(partial_grad, "replica")
    weights_out, accum_out = adagrad(weights_in, accum_in, total_grad)
    return (weights_out[None], accum_out[None])


def solution(mesh):
    placed = (
        P("mp", "replica", None, None, None),
        P("mp", None, None),
        P("mp", None),
        P("mp", "replica", None, None, None),
        P("mp", "replica", None),
    )
    return jax.shard_map(
        on_device,
        mesh=mesh,
        in_specs=placed,
        out_specs=(P("mp", None, None), P("mp", None)),
        check_vma=False,
    )
```

profile of v0, /device:TPU:2, one launch (start us, length us, event | category | flops | bytes accessed | tf_op | source)
XLA Modules:
  0.0 211.9 jit_solution(7404038184944069721)
XLA Ops:
  7.2 0.0 copy-start
  7.2 0.0 all-reduce.2.cloned.1.call-start
  7.2 3.1 %copy.16 = bf16[1,1,128,64,128]{4,2,3,1,0:T(8,128)(2,1)S(1)} copy(bf16[1,1,128,64,128]{4,3,2,1,0:T(8,128)(2,1)} %param.5) | data formatting | bytes 4194304 | tf_op args[0]
  10.3 115.6 %all_to_all.15 = bf16[128,64,128]{2,0,1:T(8,128)(2,1)S(1)} all-to-all(bf16[128,64,128]{2,0,1:T(8,128)(2,1)S(1)} %bitcast.26), channel_id=1, replica_groups=mesh['mp'=64,'replica'=8] {'mp'}, dimensions={1} | all-to-all | bytes 4194304 | tf_op jit(solution)/shard_map/all_to_all | solution.py:19
  125.9 0.0 copy-done
  125.9 0.0 copy-start.3
  126.0 0.9 fusion.2
  126.8 0.0 copy-done.3
  126.8 0.0 copy-start.2
  126.9 0.0 copy-start.1
  126.9 3.8 %fusion = f32[4,128,128]{2,0,1:T(4,128)S(1)} fusion(f32[64,128,128]{2,1,0:T(8,128)S(1)} %fusion.2, s32[64]{0:T(128)S(1)} %bitcast.30), kind=kOutput, calls=%fused_computation | convolution fusion | flops 50331904 | bytes 4456704 | tf_op jit(solution)/shard_map/tb,tre->bre/dot_general | solution.py:34
  130.7 0.7 copy.11
  131.4 0.0 all-reduce.2.cloned.1.call-update
  131.4 70.1 %all-reduce.2.cloned.1.call-done = f32[512,128]{1,0:T(8,128)} async-done(((f32[512,128]{1,0:T(8,128)}), f32[512,128]{1,0:T(8,128)}) %all-reduce.2.cloned.1.call-update) | async-done | bytes 262160 | tf_op jit(solution)/shard_map/psum | solution.py:37
  201.5 1.1 multiply_reduce_fusion
  202.6 0.0 copy-done.2
  202.6 0.6 add.26
  203.2 0.0 copy-done.1
  203.2 1.8 fusion.5
  (1 shorter events, 0.0 us)
Async XLA Ops:
  7.2 118.8 %copy-start = (bf16[1,1,64,128,128]{4,3,2,1,0:T(8,128)(2,1)S(1)}, bf16[1,1,64,128,128]{4,3,2,1,0:T(8,128)(2,1)}, u32[]{:S(2)}) copy-start(bf16[1,1,64,128,128]{4,3,2,1,0:T(8,128)(2,1)} %param.8) | copy-start | bytes 6291460
  7.2 194.3 %all-reduce.2.cloned.1.call-start = ((), (), s32[]{:S(2)}) async-start(), calls=%async_computation.1 | async-start | bytes 524288 | tf_op jit(solution)/shard_map/psum | solution.py:37
  125.9 0.9 copy-start.3
  126.8 75.8 %copy-start.2 = (f32[1,512]{1,0:T(1,128)S(1)}, f32[1,512]{1,0:T(1,128)}, u32[]{:S(2)}) copy-start(f32[1,512]{1,0:T(1,128)} %param.7) | copy-start | bytes 6148
  126.9 76.4 %copy-start.1 = (f32[1,512,128]{2,1,0:T(8,128)S(1)}, f32[1,512,128]{2,1,0:T(8,128)}, u32[]{:S(2)}) copy-start(f32[1,512,128]{2,1,0:T(8,128)} %param.6) | copy-start | bytes 786436
Sparse Core Ops, SparseCore 0:
  131.5 69.9 all-reduce.1
where the time goes:
time: 212 us
  blocking collectives  116 us (55%)
  waiting for transfers between devices  70.1 us (33%)
  between operations  14.1 us (7%)
  matrix products  4.67 us (2%)
  local copies, waits for them, and re-layouts  3.83 us (2%)
  other arithmetic  3.48 us (2%)
    all_to_all x1, blocking collectives, on_device(): lax.all_to_all(local_grads, 'mp', split_axis=1, concat_axis=0, tiled=True)  116 us
    psum x1, waiting for transfers between devices, on_device(): total_grad = lax.psum(partial_grad, 'replica')  70.1 us
  transfers between devices with their start and end apart: 1, of which 1 were waited for; matrix products, arithmetic and copies ran while one was open for 0% of the time, Pallas kernels for 0%

commit v1 on v0

--- a/solution.py
+++ b/solution.py
@@ -1,3 +1,4 @@
+import functools
 import jax
 import jax.numpy as jnp
 from jax import lax
@@ -5,6 +6,13 @@
 
 LEARN_RATE = 0.5
 EPSILON = 1e-06
+
+
+def hold_the_plate(mat, named_axis):
+    return jnp.sum(lax.all_gather(mat, named_axis), axis=0)
+
+
+map_place = functools.partial(hold_the_plate, named_axis="replica")
 
 
 def adagrad(weights_in, accum_in, gradient):
@@ -34,7 +42,7 @@
     partial_grad = jnp.einsum(
         "tb,tre->bre", onehot, contrib, precision=lax.Precision.HIGHEST
     ).reshape(row_count, width)
-    total_grad = lax.psum(partial_grad, "replica")
+    total_grad = map_place(partial_grad)
     weights_out, accum_out = adagrad(weights_in, accum_in, total_grad)
     return (weights_out[None], accum_out[None])
 

time: 212 us -> 170 us (0.80)
  the two profiles are of different devices: /device:TPU:2 before, /device:TPU:1 now
where the time goes in v1:
time: 170 us
  blocking collectives  114 us (67%)
  waiting for transfers between devices  30.7 us (18%)
  between operations  14.1 us (8%)
  matrix products  4.67 us (3%)
  local copies, waits for them, and re-layouts  3.83 us (2%)
  other arithmetic  3.3 us (2%)
    all_to_all x1, blocking collectives, on_device(): lax.all_to_all(local_grads, 'mp', split_axis=1, concat_axis=0, tiled=True)  114 us
    all_gather x1, waiting for transfers between devices, hold_the_plate(): return jnp.sum(lax.all_gather(mat, named_axis), axis=0)  30.7 us
    dot_general x1, matrix products, on_device(): jnp.einsum('tb,tre->bre', onehot, contrib, precision=lax.Precision.HIGHEST)  3.8 us
  transfers between devices with their start and end apart: 1, of which 1 were waited for; matrix products, arithmetic and copies ran while one was open for 0% of the time, Pallas kernels for 0%

profile of v1, /device:TPU:1, one launch (start us, length us, event | category | flops | bytes accessed | tf_op | source)
XLA Modules:
  0.0 170.2 jit_solution(7320788965687708744)
XLA Ops:
  7.2 0.0 copy-start
  7.2 0.0 all-gather.2.cloned.1.call-start
  7.2 3.1 %copy.16 = bf16[1,1,128,64,128]{4,2,3,1,0:T(8,128)(2,1)S(1)} copy(bf16[1,1,128,64,128]{4,3,2,1,0:T(8,128)(2,1)} %param.5) | data formatting | bytes 4194304 | tf_op args[0]
  10.3 113.6 %all_to_all.15 = bf16[128,64,128]{2,0,1:T(8,128)(2,1)S(1)} all-to-all(bf16[128,64,128]{2,0,1:T(8,128)(2,1)S(1)} %bitcast.24), channel_id=1, replica_groups=mesh['mp'=64,'replica'=8] {'mp'}, dimensions={1} | all-to-all | bytes 4194304 | tf_op jit(solution)/shard_map/all_to_all | solution.py:27
  123.9 0.0 copy-done
  123.9 0.0 copy-start.3
  123.9 0.9 fusion.2
  124.8 0.0 copy-done.3
  124.8 3.8 %fusion = f32[4,128,128]{2,0,1:T(4,128)S(1)} fusion(f32[64,128,128]{2,1,0:T(8,128)S(1)} %fusion.2, s32[64]{0:T(128)S(1)} %bitcast.28), kind=kOutput, calls=%fused_computation | convolution fusion | flops 50331904 | bytes 4456704 | tf_op jit(solution)/shard_map/tb,tre->bre/dot_general | solution.py:42
  128.6 0.0 copy-start.2
  128.6 0.0 copy-start.1
  128.6 0.7 copy.11
  129.3 0.0 all-gather.2.cloned.1.call-update
  129.3 30.7 %all-gather.2.cloned.1.call-done = f32[8,512,128]{2,1,0:T(8,128)} async-done(((f32[1,512,128]{2,1,0:T(8,128)}), f32[8,512,128]{2,1,0:T(8,128)}) %all-gather.2.cloned.1.call-update) | async-done | bytes 2097168 | tf_op jit(solution)/shard_map/all_gather | solution.py:12
  160.0 1.7 %reduce_sum.18 = f32[512,128]{1,0:T(8,128)S(1)} reduce(f32[8,512,128]{2,1,0:T(8,128)} %all-gather.2.cloned.1.call-done, f32[]{:T(128)} %constant.1.clone.1), dimensions={0}, to_apply=%region_0.0 | reduce | flops 458752 | bytes 2359300 | tf_op jit(solution)/shard_map/reduce_sum | solution.py:12
  161.7 0.1 multiply_reduce_fusion
  161.9 0.0 copy-done.2
  161.9 0.6 add.24
  162.5 0.0 copy-done.1
  162.5 0.8 fusion.5
  (1 shorter events, 0.0 us)
Async XLA Ops:
  7.2 116.7 %copy-start = (bf16[1,1,64,128,128]{4,3,2,1,0:T(8,128)(2,1)S(1)}, bf16[1,1,64,128,128]{4,3,2,1,0:T(8,128)(2,1)}, u32[]{:S(2)}) copy-start(bf16[1,1,64,128,128]{4,3,2,1,0:T(8,128)(2,1)} %param.8) | copy-start | bytes 6291460
  7.2 152.8 %all-gather.2.cloned.1.call-start = ((), (), s32[]{:S(2)}) async-start(), calls=%async_computation.1 | async-start | bytes 2359296 | tf_op jit(solution)/shard_map/all_gather | solution.py:12
  123.9 0.9 copy-start.3
  128.6 33.3 %copy-start.2 = (f32[1,512]{1,0:T(1,128)S(1)}, f32[1,512]{1,0:T(1,128)}, u32[]{:S(2)}) copy-start(f32[1,512]{1,0:T(1,128)} %param.7) | copy-start | bytes 6148
  128.6 33.9 %copy-start.1 = (f32[1,512,128]{2,1,0:T(8,128)S(1)}, f32[1,512,128]{2,1,0:T(8,128)}, u32[]{:S(2)}) copy-start(f32[1,512,128]{2,1,0:T(8,128)} %param.6) | copy-start | bytes 786436
Sparse Core Ops, SparseCore 0:
  129.5 30.5 all-gather.1
